TPU v7x, 256 devices: a whole 4x4x8 slice. The times are simulated.
256 devices in a mesh: mass: 32 (over x, z), sub: 8 (over y, core).
Axes of the slice: x: 4, y: 4, z: 8, core: 2. Of those that a mesh axis runs over, the one named last changes fastest.
Arguments:
- spectra: bfloat16 [32768, 4096], P(('mass', 'sub')), may hold values from -6 to 6
- w_in: bfloat16 [4096, 2048], P(None, 'sub'), may hold values from -0.09375 to 0.09375
- w_out: bfloat16 [2048, 512], P('sub'), may hold values from -0.125 to 0.125
- partner_rows: int32 [32, 8, 32, 8], P('mass', 'sub'), may hold values from 0 to 127
- pair_counts: int32 [32, 8, 32], P('mass', 'sub'), may hold values from 0 to 8, as said below
- pair_labels: int32 [32, 8, 32, 8], P('mass', 'sub'), may hold values from 0 to 1, as said below
Outputs:
- grad_in: float32 [4096, 2048], P('mass', 'sub')
- grad_out_t: float32 [512, 2048], P('mass', 'sub')
Inputs may be any that keep to these rules, and one draw needn't show every extreme that they name: pair_counts[m, s, q] equals pair_counts[q, s, m], is 0 for q = m, and at most 8; some count equals 8. pair_labels[m, s, q, c] equals pair_labels[q, s, m, c] for q != m.
All inputs are finite; a program needn't handle non-finite values.
Results may differ from a plain program's by a relative error of at most 0.0053.
Values may be sent and summed in bfloat16 or wider, within the bound.
A program may use at most 64 MiB of HBM per device.

v0:
```python
import jax
import jax.numpy as jnp
from jax import lax
from jax.sharding import PartitionSpec as P


def per_device(spectra, w_in, w_out, partner_rows, pair_counts, pair_labels):
    own_rows = spectra.shape[0]
    peers = partner_rows.shape[2]
    slots = partner_rows.shape[3]
    shard_rows = lax.all_gather(spectra, "sub", axis=0, tiled=True)
    pre = jnp.dot(shard_rows, w_in, preferred_element_type=jnp.float32)
    hidden = jax.nn.silu(pre).astype(jnp.bfloat16)
    embed = lax.psum_scatter(
        jnp.dot(hidden, w_out, preferred_element_type=jnp.float32),
        "sub",
        scatter_dimension=0,
        tiled=True,
    )
    norm = jnp.sqrt(jnp.sum(embed * embed, axis=-1, keepdims=True) + 1e-06)
    unit = embed / norm
    unit_b = unit.astype(jnp.bfloat16)
    flat_rows = partner_rows.reshape(peers * slots)
    selector = flat_rows[:, None] == jnp.arange(own_rows, dtype=jnp.int32)[None, :]
    mine = jnp.dot(
        selector.astype(jnp.bfloat16), unit_b, preferred_element_type=jnp.float32
    ).astype(jnp.bfloat16)
    outgoing = mine.reshape(peers, slots, mine.shape[1])
    incoming = lax.all_to_all(outgoing, "mass", split_axis=0, concat_axis=0, tiled=True)
    theirs = incoming.astype(jnp.float32)
    sim = jnp.sum(outgoing.astype(jnp.float32) * theirs, axis=-1)
    valid = jnp.arange(slots, dtype=jnp.int32)[None, :] < pair_counts.reshape(peers)[:, None]
    labels = pair_labels.reshape(peers, slots).astype(jnp.float32)
    coef = jnp.where(valid, 2.0 * (sim - labels), jnp.float32(0.0))
    weighted = (coef[..., None] * theirs).reshape(peers * slots, theirs.shape[2])
    grad_unit = lax.dot_general(
        selector.astype(jnp.float32),
        weighted,
        (((0,), (0,)), ((), ())),
        precision=lax.Precision.HIGHEST,
    )
    along = jnp.sum(unit * grad_unit, axis=-1, keepdims=True)
    grad_embed = ((grad_unit - unit * along) / norm).astype(jnp.bfloat16)
    grad_rows = lax.all_gather(grad_embed, "sub", axis=0, tiled=True)
    back = lax.dot_general(
        grad_rows, w_out, (((1,), (1,)), ((), ())), preferred_element_type=jnp.float32
    )
    gate = jax.nn.sigmoid(pre)
    grad_pre = (back * gate * (1.0 + pre * (1.0 - gate))).astype(jnp.bfloat16)
    out_part = lax.dot_general(
        grad_rows, hidden, (((0,), (0,)), ((), ())), preferred_element_type=jnp.float32
    )
    in_part = lax.dot_general(
        shard_rows, grad_pre, (((0,), (0,)), ((), ())), preferred_element_type=jnp.float32
    )
    n_mass = peers
    in_rows = in_part.shape[0] // n_mass
    out_rows = out_part.shape[0] // n_mass
    partial = jnp.concatenate(
        [
            in_part.reshape(n_mass, in_rows, in_part.shape[1]),
            out_part.reshape(n_mass, out_rows, out_part.shape[1]),
        ],
        axis=1,
    ).astype(jnp.bfloat16)
    summed = jnp.sum(
        lax.all_to_all(partial, "mass", split_axis=0, concat_axis=0, tiled=True).astype(
            jnp.float32
        ),
        axis=0,
    )
    grad_in, grad_out_t = (summed[:in_rows], summed[in_rows:])
    return (grad_in, grad_out_t)


def solution(mesh):
    placed = (
        P(("mass", "sub"), None),
        P(None, "sub"),
        P("sub", None),
        P("mass", "sub", None, None),
        P("mass", "sub", None),
        P("mass", "sub", None, None),
    )
    return jax.shard_map(
        per_device,
        mesh=mesh,
        in_specs=placed,
        out_specs=(P("mass", "sub"), P("mass", "sub")),
        check_vma=False,
    )
```

profile of v0, /device:TPU:32, one launch (start us, length us, event | category | flops | bytes accessed | tf_op | source)
XLA Modules:
  0.0 248.9 jit_solution(8469015729756273993)
XLA Ops:
  7.2 0.7 all-gather.3.cloned.1.call-update
  8.0 56.8 %all-gather.3.cloned.1.call-done = bf16[1024,4096]{1,0:T(8,128)(2,1)} async-done(((bf16[128,4096]{1,0:T(8,128)(2,1)}), bf16[1024,4096]{1,0:T(8,128)(2,1)}) %all-gather.3.cloned.1.call-update) | async-done | bytes 8388624 | tf_op jit(solution)/shard_map/all_gather | solution.py:11
  64.8 5.7 %fusion.20 = f32[1024,256]{1,0:T(8,128)S(1)} fusion(bf16[1024,4096]{1,0:T(8,128)(2,1)} %all-gather.3.cloned.1.call-done, bf16[4096,256]{1,0:T(8,128)(2,1)S(1)} %copy-done), kind=kOutput, calls=%fused_computation.37 | convolution fusion | flops 2147483648 | bytes 11534336 | tf_op jit(solution)/shard_map/dot_general | solution.py:12
  70.5 1.0 copy-done.8
  71.5 1.8 fusion.19
  73.4 0.1 eq.15
  73.5 36.3 %reduce-scatter.2.cloned.1.call-done = f32[128,512]{1,0:T(8,128)} async-done(((f32[1024,512]{1,0:T(8,128)}), f32[128,512]{1,0:T(8,128)}) %reduce-scatter.2.cloned.1.call-update) | async-done | bytes 262160 | tf_op jit(solution)/shard_map/reduce_scatter | solution.py:14
  109.9 1.1 multiply_reduce_fusion.1
  111.0 2.0 fusion.3
  113.0 10.1 %all-to-all-start = ((bf16[32,8,512]{2,1,0:T(8,128)(2,1)}), bf16[32,8,512]{2,1,0:T(8,128)(2,1)S(1)}, u32[]{:S(2)}, u32[]{:S(2)}) async-start(bf16[32,8,512]{2,1,0:T(8,128)(2,1)} %fusion.3), calls=%async_computation.1 | async-start | bytes 524288 | tf_op jit(solution)/shard_map/all_to_all | solution.py:29
  123.1 0.1 copy.14
  123.2 10.9 %all-to-all-done = bf16[32,8,512]{2,1,0:T(8,128)(2,1)S(1)} async-done(((bf16[32,8,512]{2,1,0:T(8,128)(2,1)}), bf16[32,8,512]{2,1,0:T(8,128)(2,1)S(1)}, u32[]{:S(2)}, u32[]{:S(2)}) %all-to-all-start) | async-done | bytes 262176 | tf_op jit(solution)/shard_map/all_to_all | solution.py:29
  134.1 1.1 fusion.7
  135.3 1.5 multiply_reduce_fusion
  136.8 0.8 divide_convert_fusion
  137.6 20.8 %all-gather.5.cloned.1.call-done = bf16[1024,512]{1,0:T(8,128)(2,1)} async-done(((bf16[128,512]{1,0:T(8,128)(2,1)}), bf16[1024,512]{1,0:T(8,128)(2,1)}) %all-gather.5.cloned.1.call-update) | async-done | bytes 1048592 | tf_op jit(solution)/shard_map/all_gather | solution.py:44
  158.4 8.6 %fusion = bf16[4096,256]{0,1:T(8,128)(2,1)} fusion(bf16[1024,4096]{1,0:T(8,128)(2,1)} %all-gather.3.cloned.1.call-done, bf16[1024,512]{1,0:T(8,128)(2,1)} %all-gather.5.cloned.1.call-done, bf16[256,512]{1,0:T(8,128)(2,1)S(1)} %copy-done.7, f32[1024,256]{1,0:T(8,128)} %copy-done.8), kind=kOutput, calls=%fused_computation.1 | convolution fusion | flops 2419326976 | bytes 12845056 | tf_op jit(solution)/shard_map/dot_general | solution.py:53
  167.0 4.2 %copy.19 = bf16[4096,256]{1,0:T(8,128)(2,1)} copy(bf16[4096,256]{0,1:T(8,128)(2,1)} %fusion) | data formatting | bytes 4194304 | tf_op jit(solution)/shard_map/reshape | solution.py:61
  171.2 1.9 convolution_convert_fusion.1
  173.1 0.2 pad_maximum_fusion
  173.3 67.5 %all_to_all.10 = bf16[32,144,256]{2,1,0:T(8,128)(2,1)S(1)} all-to-all(bf16[32,144,256]{2,1,0:T(8,128)(2,1)S(1)} %pad_maximum_fusion), channel_id=1, replica_groups=mesh['mass'=32,'sub'=8] {'mass'}, dimensions={0} | all-to-all | bytes 4718592 | tf_op jit(solution)/shard_map/all_to_all | solution.py:67
  240.8 0.3 convert_reduce_fusion
  241.1 0.6 slice.9
  241.7 0.7 slice.8
  (25 shorter events, 0.3 us)
Async XLA Ops:
  7.2 57.6 %copy-start = (bf16[4096,256]{1,0:T(8,128)(2,1)S(1)}, bf16[4096,256]{1,0:T(8,128)(2,1)}, u32[]{:S(2)}) copy-start(bf16[4096,256]{1,0:T(8,128)(2,1)} %param.7) | copy-start | bytes 6291460
  7.2 57.6 %all-gather.3.cloned.1.call-start = ((), (), s32[]{:S(2)}) async-start(), calls=%async_computation.3 | async-start | bytes 9437184 | tf_op jit(solution)/shard_map/all_gather | solution.py:11
  7.9 63.6 %copy-start.7 = (bf16[256,512]{1,0:T(8,128)(2,1)S(1)}, bf16[256,512]{1,0:T(8,128)(2,1)}, u32[]{:S(2)}) copy-start(bf16[256,512]{1,0:T(8,128)(2,1)} %param.8) | copy-start | bytes 786436
  7.9 102.0 %reduce-scatter.2.cloned.1.call-start = ((), (), s32[]{:S(2)}) async-start(), calls=%async_computation.4 | async-start | bytes 2359296 | tf_op jit(solution)/shard_map/reduce_scatter | solution.py:14
  70.5 1.0 copy-start.8
  71.5 1.9 copy-start.3
  73.3 49.8 %copy-start.4 = (s32[1,1,32,8]{2,3,1,0:T(8,128)S(1)}, s32[1,1,32,8]{2,3,1,0:T(8,128)}, u32[]{:S(2)}) copy-start(s32[1,1,32,8]{2,3,1,0:T(8,128)} %param.11) | copy-start | bytes 3076
  73.3 61.9 %copy-start.5 = (s32[1,1,32]{2,1,0:T(1,128)S(1)}, s32[1,1,32]{2,1,0:T(1,128)}, u32[]{:S(2)}) copy-start(s32[1,1,32]{2,1,0:T(1,128)} %param.10) | copy-start | bytes 388
  109.9 26.9 %copy-start.2 = (f32[128,512]{1,0:T(8,128)S(1)}, f32[128,512]{1,0:T(8,128)}, u32[]{:S(2)}) copy-start(f32[128,512]{1,0:T(8,128)} %reduce-scatter.2.cloned.1.call-done) | copy-start | bytes 786436
  113.0 21.1 %all-to-all-start = ((bf16[32,8,512]{2,1,0:T(8,128)(2,1)}), bf16[32,8,512]{2,1,0:T(8,128)(2,1)S(1)}, u32[]{:S(2)}, u32[]{:S(2)}) async-start(bf16[32,8,512]{2,1,0:T(8,128)(2,1)} %fusion.3), calls=%async_computation.1 | async-start | bytes 524288 | tf_op jit(solution)/shard_map/all_to_all | solution.py:29
  123.1 35.3 %all-gather.5.cloned.1.call-start = ((), (), s32[]{:S(2)}) async-start(), calls=%async_computation.5 | async-start | bytes 1179648 | tf_op jit(solution)/shard_map/all_gather | solution.py:44
  167.0 4.2 %copy-start.6 = (bf16[1024,512]{1,0:T(8,128)(2,1)S(1)}, bf16[1024,512]{1,0:T(8,128)(2,1)}, u32[]{:S(2)}) copy-start(bf16[1024,512]{1,0:T(8,128)(2,1)} %all-gather.5.cloned.1.call-done) | copy-start | bytes 3145732
  171.2 2.0 copy-start.1
Sparse Core Ops, SparseCore 0:
  9.9 54.8 all-gather.2
  73.5 36.3 reduce-scatter.1
  137.7 20.6 all-gather.4
where the time goes:
time: 249 us
  waiting for transfers between devices  126 us (51%)
  blocking collectives  67.5 us (27%)
  matrix products  21.5 us (9%)
  between operations  13.9 us (6%)
  starting transfers between devices  10.2 us (4%)
  local copies, waits for them, and re-layouts  6.69 us (3%)
  other arithmetic  3.58 us (1%)
    all_to_all x1, blocking collectives, per_device(): lax.all_to_all(partial, 'mass', split_axis=0, concat_axis=0, tiled=True)  67.5 us
    all_gather x1, waiting for transfers between devices, per_device(): shard_rows = lax.all_gather(spectra, 'sub', axis=0, tiled=True)  56.8 us
    reduce_scatter x1, waiting for transfers between devices, per_device(): lax.psum_scatter(jnp.dot(hidden, w_out, preferred_element_type=jnp.float3...  36.3 us
    all_gather x1, waiting for transfers between devices, per_device(): grad_rows = lax.all_gather(grad_embed, 'sub', axis=0, tiled=True)  20.8 us
    all_to_all x1, waiting for transfers between devices, per_device(): lax.all_to_all(outgoing, 'mass', split_axis=0, concat_axis=0, tiled=True)  10.9 us
    all_to_all x1, starting transfers between devices, per_device(): lax.all_to_all(outgoing, 'mass', split_axis=0, concat_axis=0, tiled=True)  10.1 us
    dot_general x1, matrix products, per_device(): lax.dot_general(shard_rows, grad_pre, (((0,), (0,)), ((), ())), preferred...  8.59 us
    dot_general x1, matrix products, per_device(): pre = jnp.dot(shard_rows, w_in, preferred_element_type=jnp.float32)  5.71 us
  transfers between devices with their start and end apart: 4, of which 4 were waited for; matrix products, arithmetic and copies ran while one was open for 0% of the time, Pallas kernels for 0%

commit v1 on v0

--- a/solution.py
+++ b/solution.py
@@ -1,7 +1,21 @@
+import functools
 import jax
 import jax.numpy as jnp
 from jax import lax
 from jax.sharding import PartitionSpec as P
+
+
+def _update_notes(sample, across):
+    carry_out = jnp.concatenate(
+        lax.all_to_all(
+            jnp.stack([sample for _ in range(lax.axis_size(across))], axis=0), across, 0, 0
+        ),
+        0,
+    )
+    return carry_out
+
+
+thing_edit = functools.partial(_update_notes, across="sub")
 
 
 def per_device(spectra, w_in, w_out, partner_rows, pair_counts, pair_labels):
@@ -41,7 +55,7 @@
     )
     along = jnp.sum(unit * grad_unit, axis=-1, keepdims=True)
     grad_embed = ((grad_unit - unit * along) / norm).astype(jnp.bfloat16)
-    grad_rows = lax.all_gather(grad_embed, "sub", axis=0, tiled=True)
+    grad_rows = thing_edit(grad_embed)
     back = lax.dot_general(
         grad_rows, w_out, (((1,), (1,)), ((), ())), preferred_element_type=jnp.float32
     )

time: 249 us -> 244 us (0.980)
  waiting for transfers between devices: 126 us -> 105 us
  blocking collectives: 67.5 us -> 80.4 us
  local copies, waits for them, and re-layouts: 6.69 us -> 9.65 us
    all_gather x1 -> x0, waiting for transfers between devices: 20.8 us -> none  [per_device(): grad_rows = lax.all_gather(grad_embed, 'sub', axis=0, tiled=True)]
    all_to_all x0 -> x1, blocking collectives: none -> 19.2 us  [_update_notes(): lax.all_to_all(jnp.stack([sample for _ in range(lax.axis_size(across))],...]
    all_to_all x1, blocking collectives: 67.5 us -> 61.2 us  [per_device(): lax.all_to_all(partial, 'mass', split_axis=0, concat_axis=0, tiled=True)]
  transfers between devices with their start and end apart: 4 -> 3, of which waited for: 4 -> 3; matrix products, arithmetic and copies ran while one was open for 0% -> 0% of each run, Pallas kernels for 0% -> 0%
where the time goes in v1:
time: 244 us
  waiting for transfers between devices  105 us (43%)
  blocking collectives  80.4 us (33%)
  matrix products  21.5 us (9%)
  between operations  14.2 us (6%)
  starting transfers between devices  10.2 us (4%)
  local copies, waits for them, and re-layouts  9.65 us (4%)
  other arithmetic  2.92 us (1%)
    all_to_all x1, blocking collectives, per_device(): lax.all_to_all(partial, 'mass', split_axis=0, concat_axis=0, tiled=True)  61.2 us
    all_gather x1, waiting for transfers between devices, per_device(): shard_rows = lax.all_gather(spectra, 'sub', axis=0, tiled=True)  56.8 us
    reduce_scatter x1, waiting for transfers between devices, per_device(): lax.psum_scatter(jnp.dot(hidden, w_out, preferred_element_type=jnp.float3...  36.3 us
    all_to_all x1, blocking collectives, _update_notes(): lax.all_to_all(jnp.stack([sample for _ in range(lax.axis_size(across))],...  19.2 us
    all_to_all x1, waiting for transfers between devices, per_device(): lax.all_to_all(outgoing, 'mass', split_axis=0, concat_axis=0, tiled=True)  11 us
    all_to_all x1, starting transfers between devices, per_device(): lax.all_to_all(outgoing, 'mass', split_axis=0, concat_axis=0, tiled=True)  10.1 us
    dot_general x1, matrix products, per_device(): lax.dot_general(shard_rows, grad_pre, (((0,), (0,)), ((), ())), preferred...  8.29 us
    dot_general x1, matrix products, per_device(): pre = jnp.dot(shard_rows, w_in, preferred_element_type=jnp.float32)  5.71 us
  transfers between devices with their start and end apart: 3, of which 3 were waited for; matrix products, arithmetic and copies ran while one was open for 0% of the time, Pallas kernels for 0%

profile of v1, /device:TPU:32, one launch (start us, length us, event | category | flops | bytes accessed | tf_op | source)
XLA Modules:
  0.0 243.7 jit_solution(2869712950035792500)
XLA Ops:
  7.2 0.7 all-gather.2.cloned.1.call-update
  8.0 56.8 %all-gather.2.cloned.1.call-done = bf16[1024,4096]{1,0:T(8,128)(2,1)} async-done(((bf16[128,4096]{1,0:T(8,128)(2,1)}), bf16[1024,4096]{1,0:T(8,128)(2,1)}) %all-gather.2.cloned.1.call-update) | async-done | bytes 8388624 | tf_op jit(solution)/shard_map/all_gather | solution.py:25
  64.8 5.7 %fusion.21 = f32[1024,256]{1,0:T(8,128)S(1)} fusion(bf16[1024,4096]{1,0:T(8,128)(2,1)} %all-gather.2.cloned.1.call-done, bf16[4096,256]{1,0:T(8,128)(2,1)S(1)} %copy-done), kind=kOutput, calls=%fused_computation.38 | convolution fusion | flops 2147483648 | bytes 11534336 | tf_op jit(solution)/shard_map/dot_general | solution.py:26
  70.5 1.0 copy-done.7
  71.5 1.8 fusion.20
  73.6 36.3 %reduce-scatter.2.cloned.1.call-done = f32[128,512]{1,0:T(8,128)} async-done(((f32[1024,512]{1,0:T(8,128)}), f32[128,512]{1,0:T(8,128)}) %reduce-scatter.2.cloned.1.call-update) | async-done | bytes 262160 | tf_op jit(solution)/shard_map/reduce_scatter | solution.py:28
  109.9 1.1 multiply_reduce_fusion.1
  111.0 2.0 fusion.3
  113.0 10.1 %all-to-all-start = ((bf16[32,8,512]{2,1,0:T(8,128)(2,1)}), bf16[32,8,512]{2,1,0:T(8,128)(2,1)S(1)}, u32[]{:S(2)}, u32[]{:S(2)}) async-start(bf16[32,8,512]{2,1,0:T(8,128)(2,1)} %fusion.3), calls=%async_computation.1 | async-start | bytes 524288 | tf_op jit(solution)/shard_map/all_to_all | solution.py:43
  123.2 11.0 %all-to-all-done = bf16[32,8,512]{2,1,0:T(8,128)(2,1)S(1)} async-done(((bf16[32,8,512]{2,1,0:T(8,128)(2,1)}), bf16[32,8,512]{2,1,0:T(8,128)(2,1)S(1)}, u32[]{:S(2)}, u32[]{:S(2)}) %all-to-all-start) | async-done | bytes 262176 | tf_op jit(solution)/shard_map/all_to_all | solution.py:43
  134.1 1.1 fusion.7
  135.3 1.5 multiply_reduce_fusion
  137.0 0.1 stack.2
  137.2 19.2 %all_to_all.15 = bf16[8,128,512]{1,2,0:T(8,128)(2,1)} all-to-all(bf16[8,128,512]{1,2,0:T(8,128)(2,1)S(1)} %stack.2), channel_id=1, replica_groups=mesh['mass'=32,'sub'=8] {'sub'}, dimensions={0} | all-to-all | bytes 2097152 | tf_op jit(solution)/shard_map/all_to_all | solution.py:10
  156.4 1.5 copy.25
  157.9 8.3 %fusion = bf16[4096,256]{0,1:T(8,128)(2,1)} fusion(bf16[1024,4096]{1,0:T(8,128)(2,1)} %all-gather.2.cloned.1.call-done, bf16[1024,512]{1,0:T(8,128)(2,1)S(1)} %bitcast.34, bf16[256,512]{1,0:T(8,128)(2,1)S(1)} %copy-done.6, f32[1024,256]{1,0:T(8,128)} %copy-done.7), kind=kOutput, calls=%fused_computation.1 | convolution fusion | flops 2419326976 | bytes 12845056 | tf_op jit(solution)/shard_map/dot_general | solution.py:67
  166.2 4.1 %copy.31 = bf16[4096,256]{1,0:T(8,128)(2,1)} copy(bf16[4096,256]{0,1:T(8,128)(2,1)} %fusion) | data formatting | bytes 4194304 | tf_op jit(solution)/shard_map/reshape | solution.py:75
  170.3 1.3 copy.26
  171.6 2.2 convolution_convert_fusion.1
  173.9 0.2 pad_maximum_fusion
  174.0 61.2 %all_to_all.16 = bf16[32,144,256]{2,1,0:T(8,128)(2,1)S(1)} all-to-all(bf16[32,144,256]{2,1,0:T(8,128)(2,1)S(1)} %pad_maximum_fusion), channel_id=1, replica_groups=mesh['mass'=32,'sub'=8] {'mass'}, dimensions={0} | all-to-all | bytes 4718592 | tf_op jit(solution)/shard_map/all_to_all | solution.py:81
  235.2 0.3 convert_reduce_fusion
  235.6 0.6 slice.9
  236.2 0.7 slice.8
  (25 shorter events, 0.7 us)
Async XLA Ops:
  7.2 57.6 %copy-start = (bf16[4096,256]{1,0:T(8,128)(2,1)S(1)}, bf16[4096,256]{1,0:T(8,128)(2,1)}, u32[]{:S(2)}) copy-start(bf16[4096,256]{1,0:T(8,128)(2,1)} %param.7) | copy-start | bytes 6291460
  7.2 57.6 %all-gather.2.cloned.1.call-start = ((), (), s32[]{:S(2)}) async-start(), calls=%async_computation.4 | async-start | bytes 9437184 | tf_op jit(solution)/shard_map/all_gather | solution.py:25
  7.9 63.6 %copy-start.6 = (bf16[256,512]{1,0:T(8,128)(2,1)S(1)}, bf16[256,512]{1,0:T(8,128)(2,1)}, u32[]{:S(2)}) copy-start(bf16[256,512]{1,0:T(8,128)(2,1)} %param.8) | copy-start | bytes 786436
  7.9 101.9 %reduce-scatter.2.cloned.1.call-start = ((), (), s32[]{:S(2)}) async-start(), calls=%async_computation.5 | async-start | bytes 2359296 | tf_op jit(solution)/shard_map/reduce_scatter | solution.py:28
  70.5 1.0 copy-start.7
  71.5 1.9 copy-start.3
  73.3 49.7 %copy-start.4 = (s32[1,1,32,8]{2,3,1,0:T(8,128)S(1)}, s32[1,1,32,8]{2,3,1,0:T(8,128)}, u32[]{:S(2)}) copy-start(s32[1,1,32,8]{2,3,1,0:T(8,128)} %param.11) | copy-start | bytes 3076
  73.4 61.9 %copy-start.5 = (s32[1,1,32]{2,1,0:T(1,128)S(1)}, s32[1,1,32]{2,1,0:T(1,128)}, u32[]{:S(2)}) copy-start(s32[1,1,32]{2,1,0:T(1,128)} %param.10) | copy-start | bytes 388
  109.9 26.9 %copy-start.2 = (f32[128,512]{1,0:T(8,128)S(1)}, f32[128,512]{1,0:T(8,128)}, u32[]{:S(2)}) copy-start(f32[128,512]{1,0:T(8,128)} %reduce-scatter.2.cloned.1.call-done) | copy-start | bytes 786436
  113.0 21.1 %all-to-all-start = ((bf16[32,8,512]{2,1,0:T(8,128)(2,1)}), bf16[32,8,512]{2,1,0:T(8,128)(2,1)S(1)}, u32[]{:S(2)}, u32[]{:S(2)}) async-start(bf16[32,8,512]{2,1,0:T(8,128)(2,1)} %fusion.3), calls=%async_computation.1 | async-start | bytes 524288 | tf_op jit(solution)/shard_map/all_to_all | solution.py:43
  171.6 2.3 copy-start.1
Sparse Core Ops, SparseCore 0:
  9.9 54.8 all-gather.1
  73.5 36.3 reduce-scatter.1
